TPU v7x, 256 devices: a whole 4x4x8 slice. The times are simulated.
256 devices in a mesh: expert: 8 (over x, core), dp: 8 (over z), pipe: 4 (over y).
Axes of the slice: x: 4, y: 4, z: 8, core: 2. Of those that a mesh axis runs over, the one named last changes fastest.
Arguments:
- tokens: bfloat16 [2048, 3072], P(('expert', 'dp'), 'pipe'), may hold values from -6 to 6
- out_grad: bfloat16 [2048, 3072], P(('expert', 'dp'), 'pipe'), may hold values from -6 to 6
- gate_values: float32 [2048, 2], P(('expert', 'dp')), may hold values from 0.1 to 1
- expert_ids: int32 [2048, 2], P(('expert', 'dp')), may hold values from 0 to 7, all different within a row; in each aligned block of 32 rows (0 to 31, 32 to 63, ...) at most 16 rows name the same one
- w_gate: bfloat16 [8, 3072, 8192], P('expert', None, ('dp', 'pipe')), may hold values from -0.109375 to 0.109375
- w_up: bfloat16 [8, 3072, 8192], P('expert', None, ('dp', 'pipe')), may hold values from -0.109375 to 0.109375
- w_down: bfloat16 [8, 8192, 3072], P('expert', ('dp', 'pipe')), may hold values from -0.0625 to 0.0625
Outputs:
- grad_tokens: bfloat16 [2048, 3072], P(('expert', 'dp'), 'pipe')
- gate_weight_gradient: bfloat16 [8, 3072, 8192], P('expert', None, ('dp', 'pipe'))
- up_weight_gradient: bfloat16 [8, 3072, 8192], P('expert', None, ('dp', 'pipe'))
- grad_down: bfloat16 [8, 8192, 3072], P('expert', ('dp', 'pipe'))
Inputs may be any that keep to these rules, and one draw needn't show every extreme that they name: `expert_ids`: each token names two different experts; among the 32 tokens of one block no expert is named more than 16 times, and in some blocks one is named exactly 16 times.
All inputs are finite; a program needn't handle non-finite values.
Results may differ from a plain program's by a relative error of at most 0.0065.
Values may be sent and summed in bfloat16 or wider, within the bound.
No kernel may reach another device: no remote copies, remote signals or barrier semaphores. Data moves between devices by JAX's collectives and lax.ppermute only.
A program may use at most 128 MiB of HBM per device.

v0:
```python
import jax
import jax.numpy as jnp
from jax import lax
from jax.sharding import PartitionSpec as P


def dispatch_tables(expert_ids, gate_values, expert_count, capacity):
    token_count = expert_ids.shape[0]
    choices_flat = expert_ids.reshape(-1)
    one_hot = (choices_flat[:, None] == jnp.arange(expert_count, dtype=jnp.int32)[None, :]).astype(
        jnp.int32
    )
    ranks = jnp.cumsum(one_hot, axis=0) - 1
    slot_index = choices_flat * capacity + jnp.sum(one_hot * ranks, axis=1)
    hits = jnp.arange(expert_count * capacity, dtype=jnp.int32)[:, None] == slot_index[None, :]
    hits = hits.reshape(expert_count * capacity, token_count, 2)
    picker = jnp.any(hits, axis=2).astype(jnp.bfloat16)
    weighting = jnp.sum(jnp.where(hits, gate_values[None, :, :], 0.0), axis=2)
    return (picker, weighting)


def fill_slots(picker, weighting, features, cotangent):
    sent_rows = jnp.dot(picker, features, preferred_element_type=jnp.float32).astype(jnp.bfloat16)
    sent_grads = jnp.dot(
        weighting, cotangent.astype(jnp.float32), precision=lax.Precision.HIGHEST
    ).astype(jnp.bfloat16)
    return (sent_rows, sent_grads)


def body(tokens, out_grad, gate_values, expert_ids, w_gate, w_up, w_down):
    expert_count = lax.axis_size("expert")
    group_count = lax.axis_size("dp")
    pipe_count = lax.axis_size("pipe")
    token_count = tokens.shape[0]
    capacity = max(token_count // 2, 2 * token_count // expert_count)
    slot_total = expert_count * capacity
    feat_part = tokens.shape[1]
    model_width = feat_part * pipe_count
    hidden_part = w_gate.shape[2]
    picker, weighting = dispatch_tables(expert_ids, gate_values, expert_count, capacity)
    sent_rows, sent_grads = fill_slots(picker, weighting, tokens, out_grad)
    recv_rows, recv_grads = (
        lax.all_to_all(
            sent_rows.reshape(expert_count, capacity, feat_part),
            "expert",
            split_axis=0,
            concat_axis=0,
            tiled=True,
        ),
        lax.all_to_all(
            sent_grads.reshape(expert_count, capacity, feat_part),
            "expert",
            split_axis=0,
            concat_axis=0,
            tiled=True,
        ),
    )
    gathered_rows, gathered_gradients = (
        lax.all_gather(
            recv_rows.reshape(1, slot_total, feat_part), ("dp", "pipe"), axis=0, tiled=True
        ),
        lax.all_gather(
            recv_grads.reshape(1, slot_total, feat_part), ("dp", "pipe"), axis=0, tiled=True
        ),
    )
    piece_width = model_width // pipe_count
    gathered_rows = gathered_rows.reshape(group_count, pipe_count, slot_total, piece_width)
    gathered_gradients = gathered_gradients.reshape(
        group_count, pipe_count, slot_total, piece_width
    )
    gate_weight_blocks = w_gate[0].reshape(pipe_count, piece_width, hidden_part)
    up_weight_blocks = w_up[0].reshape(pipe_count, piece_width, hidden_part)
    down_weight_blocks = w_down[0].reshape(hidden_part, pipe_count, piece_width)
    gate_pre = jnp.einsum(
        "lxvk,xkh->lvh", gathered_rows, gate_weight_blocks, preferred_element_type=jnp.float32
    )
    up_preactivation = jnp.einsum(
        "lxvk,xkh->lvh", gathered_rows, up_weight_blocks, preferred_element_type=jnp.float32
    )
    act_grad = jnp.einsum(
        "mzyj,uzj->myu", gathered_gradients, down_weight_blocks, preferred_element_type=jnp.float32
    )
    sigmoid_gate = jax.nn.sigmoid(gate_pre)
    linear = gate_pre * sigmoid_gate
    swiglu_activation = (linear * up_preactivation).astype(jnp.bfloat16)
    slope_term = sigmoid_gate * (1.0 + gate_pre * (1.0 - sigmoid_gate))
    gate_output_gradient = (act_grad * up_preactivation * slope_term).astype(jnp.bfloat16)
    up_output_gradient = (act_grad * linear).astype(jnp.bfloat16)
    gate_weight_gradient = jnp.einsum(
        "kctx,ktn->cxn", gathered_rows, gate_output_gradient, preferred_element_type=jnp.float32
    )
    gate_weight_gradient = gate_weight_gradient.reshape(model_width, hidden_part).astype(
        jnp.bfloat16
    )[None]
    up_weight_gradient = jnp.einsum(
        "kctx,ktn->cxn", gathered_rows, up_output_gradient, preferred_element_type=jnp.float32
    )
    up_weight_gradient = up_weight_gradient.reshape(model_width, hidden_part).astype(jnp.bfloat16)[
        None
    ]
    grad_down = jnp.einsum(
        "cjb,cvji->bvi", swiglu_activation, gathered_gradients, preferred_element_type=jnp.float32
    )
    grad_down = grad_down.reshape(hidden_part, model_width).astype(jnp.bfloat16)[None]
    gate_backward = w_gate[0].reshape(pipe_count, feat_part, hidden_part)
    up_backward = w_up[0].reshape(pipe_count, feat_part, hidden_part)
    input_terms = jnp.einsum(
        "mil,xkl->mxik", gate_output_gradient, gate_backward, preferred_element_type=jnp.float32
    ) + jnp.einsum(
        "mil,xkl->mxik", up_output_gradient, up_backward, preferred_element_type=jnp.float32
    )
    summed = lax.psum_scatter(
        input_terms.reshape(group_count * pipe_count, slot_total, feat_part),
        ("dp", "pipe"),
        scatter_dimension=0,
        tiled=True,
    )
    slot_grads = summed.astype(jnp.bfloat16).reshape(expert_count, capacity, feat_part)
    returned = lax.all_to_all(slot_grads, "expert", split_axis=0, concat_axis=0, tiled=True)
    grad_tokens = jnp.einsum(
        "st,sq->tq",
        picker,
        returned.reshape(slot_total, feat_part),
        preferred_element_type=jnp.float32,
    ).astype(jnp.bfloat16)
    return (grad_tokens, gate_weight_gradient, up_weight_gradient, grad_down)


def solution(mesh):
    placed = (
        P(("expert", "dp"), "pipe"),
        P(("expert", "dp"), "pipe"),
        P(("expert", "dp"), None),
        P(("expert", "dp"), None),
        P("expert", None, ("dp", "pipe")),
        P("expert", None, ("dp", "pipe")),
        P("expert", ("dp", "pipe"), None),
    )
    return jax.shard_map(
        body,
        mesh=mesh,
        in_specs=placed,
        out_specs=(
            P(("expert", "dp"), "pipe"),
            P("expert", None, ("dp", "pipe")),
            P("expert", None, ("dp", "pipe")),
            P("expert", ("dp", "pipe"), None),
        ),
        check_vma=False,
    )
```

profile of v0, /device:TPU:1, one launch (start us, length us, event | category | flops | bytes accessed | tf_op | source)
XLA Modules:
  0.0 471.8 jit_solution(10820452683716536585)
XLA Ops:
  7.2 0.0 copy-start
  7.2 0.0 all-gather.5.cloned.1.call-start
  7.2 0.9 copy.50
  8.1 0.1 eq.30
  8.2 0.1 fusion.17
  8.3 0.1 reduce_window_sum.11
  8.4 0.2 select_reduce_fusion.1
  8.6 0.1 reduce_sum.21
  8.7 0.1 copy.51
  8.8 0.7 multiply_add_fusion
  9.4 0.1 fusion.18
  9.5 1.1 convolution_convert_fusion
  10.6 12.1 %all_to_all.15 = bf16[8,16,768]{2,1,0:T(8,128)(2,1)} all-to-all(bf16[8,16,768]{2,1,0:T(8,128)(2,1)S(1)} %bitcast.111), channel_id=1, replica_groups=mesh['expert'=8,'dp'=8,'pipe'=4] {'expert'}, dimensions={0} | all-to-all | bytes 393216 | tf_op jit(solution)/shard_map/all_to_all | solution.py:43
  22.7 0.0 all-gather.5.cloned.1.call-update
  22.7 0.0 all-gather.3.cloned.1.call-start
  22.8 0.8 select_reduce_fusion
  23.5 1.2 convolution_convert_fusion.1
  24.7 9.9 %all_to_all.16 = bf16[8,16,768]{2,1,0:T(8,128)(2,1)} all-to-all(bf16[8,16,768]{2,1,0:T(8,128)(2,1)S(1)} %bitcast.110), channel_id=1, replica_groups=mesh['expert'=8,'dp'=8,'pipe'=4] {'expert'}, dimensions={0} | all-to-all | bytes 393216 | tf_op jit(solution)/shard_map/all_to_all | solution.py:50
  34.6 0.0 all-gather.3.cloned.1.call-update
  34.6 0.0 reduce-scatter.2.cloned.1.call-start
  34.7 3.3 reshape_squeeze.11
  38.0 73.0 %all-gather.5.cloned.1.call-done = bf16[32,128,768]{2,1,0:T(8,128)(2,1)} async-done(((bf16[1,128,768]{2,1,0:T(8,128)(2,1)}), bf16[32,128,768]{2,1,0:T(8,128)(2,1)}) %all-gather.5.cloned.1.call-update) | async-done | bytes 6291472 | tf_op jit(solution)/shard_map/all_gather | solution.py:59
  111.0 0.0 copy-done
  111.0 5.7 %convolution_bitcast_fusion.3 = f32[8,128,256]{2,1,0:T(8,128)} fusion(bf16[8,4,128,768]{3,2,1,0:T(8,128)(2,1)} %bitcast.97, bf16[4,768,256,1]{2,1,0,3:T(8,128)(2,1)S(1)} %bitcast.94), kind=kOutput, calls=%fused_computation.14 | convolution fusion | flops 1610612736 | bytes 8912896 | tf_op jit(solution)/shard_map/lxvk,xkh->lvh/dot_general | solution.py:74
  116.7 2.8 convolution_bitcast_fusion.4
  119.4 79.2 %all-gather.3.cloned.1.call-done = bf16[32,128,768]{2,1,0:T(8,128)(2,1)} async-done(((bf16[1,128,768]{2,1,0:T(8,128)(2,1)}), bf16[32,128,768]{2,1,0:T(8,128)(2,1)}) %all-gather.3.cloned.1.call-update) | async-done | bytes 6291472 | tf_op jit(solution)/shard_map/all_gather | solution.py:62
  198.7 5.4 %multiply_convert_fusion.1 = (bf16[8,128,256]{2,1,0:T(8,128)(2,1)S(1)}, bf16[8,128,256]{2,1,0:T(8,128)(2,1)S(1)}) fusion(f32[8,128,256]{2,1,0:T(8,128)} %convolution_bitcast_fusion.3, f32[8,128,256]{2,1,0:T(8,128)} %convolution_bitcast_fusion.4, bf16[8,4,128,768]{3,2,1,0:T(8,128)(2,1)} %bitcast.100, bf16[256,4,768]{2,1,0:T(4,128)(2,1)S(1)} %reshape_squeeze.11), kind=kOutput, calls=%fused_computation.20 | convolution fusion | flops 1614020608 | bytes 11010048 | tf_op jit(solution)/shard_map/mzyj,uzj->myu/dot_general | solution.py:80
  204.1 0.0 copy-start.7
  204.1 0.0 copy-start.4
  204.1 1.8 fusion.14
  205.9 0.0 copy-done.5
  205.9 0.0 copy-done.7
  206.0 0.0 copy-done.4
  206.0 6.4 %convolution_add_fusion = f32[8,128,4,768]{3,1,2,0:T(8,128)} fusion(f32[8,128,4,768]{3,1,2,0:T(8,128)S(1)} %fusion.14, bf16[4,768,256,1]{2,1,0,3:T(8,128)(2,1)S(1)} %bitcast.106, bf16[8,128,256]{2,1,0:T(8,128)(2,1)S(1)} %get-tuple-element.4), kind=kOutput, calls=%fused_computation | convolution fusion | flops 1613758464 | bytes 27262976 | tf_op jit(solution)/shard_map/mil,xkl->mxik/dot_general | solution.py:109
  212.3 0.0 reduce-scatter.2.cloned.1.call-update
  212.3 8.6 %copy.65 = bf16[4,768,8,128]{3,1,0,2:T(8,128)(2,1)} copy(bf16[4,768,8,128]{1,3,0,2:T(8,128)(2,1)} %bitcast.98) | data formatting | bytes 12582912 | tf_op jit(solution)/shard_map/kctx,ktn->cxn/dot_general | solution.py:89
  220.9 8.8 %copy.67 = bf16[4,768,8,128]{3,1,0,2:T(8,128)(2,1)} copy(bf16[4,768,8,128]{1,3,0,2:T(8,128)(2,1)} %bitcast.101) | data formatting | bytes 12582912 | tf_op jit(solution)/shard_map/cjb,cvji->bvi/dot_general | solution.py:101
  229.7 0.0 copy-start.10
  229.7 7.5 %fusion.4 = bf16[1,3072,256]{2,1,0:T(8,128)(2,1)} fusion(bf16[3072,8,128]{2,0,1:T(8,128)(2,1)} %bitcast.102, bf16[8,128,256]{2,1,0:T(8,128)(2,1)S(1)} %copy-done.8), kind=kOutput, calls=%fused_computation.8 | convolution fusion | flops 1611399168 | bytes 8388608 | tf_op jit(solution)/shard_map/kctx,ktn->cxn/dot_general | solution.py:95
  237.2 0.0 copy-done.10
  237.2 3.1 fusion.3
  240.3 206.2 %reduce-scatter.2.cloned.1.call-done = f32[1,128,768]{2,1,0:T(8,128)} async-done(((f32[32,128,768]{2,1,0:T(8,128)}), f32[1,128,768]{2,1,0:T(8,128)}) %reduce-scatter.2.cloned.1.call-update) | async-done | bytes 393232 | tf_op jit(solution)/shard_map/reduce_scatter | solution.py:112
  446.5 1.7 convert_element_type.40
  448.2 9.1 %all-to-all-start.2 = ((bf16[8,16,768]{2,1,0:T(8,128)(2,1)}), bf16[8,16,768]{2,1,0:T(8,128)(2,1)S(1)}, u32[]{:S(2)}, u32[]{:S(2)}) async-start(bf16[8,16,768]{2,1,0:T(8,128)(2,1)} %bitcast.24), calls=%async_computation.3 | async-start | bytes 393216 | tf_op jit(solution)/shard_map/all_to_all | solution.py:119
  457.3 0.0 copy-done.6
  457.3 7.3 %fusion.5 = bf16[1,3072,256]{2,1,0:T(8,128)(2,1)} fusion(bf16[3072,8,128]{2,0,1:T(8,128)(2,1)} %bitcast.103, bf16[8,128,256]{2,1,0:T(8,128)(2,1)S(1)} %copy-done.6), kind=kOutput, calls=%fused_computation.9 | convolution fusion | flops 1611399168 | bytes 8388608 | tf_op jit(solution)/shard_map/kctx,ktn->cxn/dot_general | solution.py:89
  464.5 0.0 all-to-all-done.2
  464.5 0.8 convolution_convert_fusion.2
  (12 shorter events, 0.0 us)
Async XLA Ops:
  7.2 103.8 %copy-start = (bf16[1,3072,256]{2,1,0:T(8,128)(2,1)S(1)}, bf16[1,3072,256]{2,1,0:T(8,128)(2,1)}, u32[]{:S(2)}) copy-start(bf16[1,3072,256]{2,1,0:T(8,128)(2,1)} %param.11) | copy-start | bytes 4718596
  7.2 103.8 %all-gather.5.cloned.1.call-start = ((), (), s32[]{:S(2)}) async-start(), calls=%async_computation.5 | async-start | bytes 6488064 | tf_op jit(solution)/shard_map/all_gather | solution.py:59
  22.7 176.0 %all-gather.3.cloned.1.call-start = ((), (), s32[]{:S(2)}) async-start(), calls=%async_computation.4 | async-start | bytes 6488064 | tf_op jit(solution)/shard_map/all_gather | solution.py:62
  34.6 411.9 %reduce-scatter.2.cloned.1.call-start = ((), (), s32[]{:S(2)}) async-start(), calls=%async_computation.6 | async-start | bytes 12976128 | tf_op jit(solution)/shard_map/reduce_scatter | solution.py:112
  111.0 5.7 %copy-start.1 = (bf16[32,128,768]{2,1,0:T(8,128)(2,1)S(1)}, bf16[32,128,768]{2,1,0:T(8,128)(2,1)}, u32[]{:S(2)}) copy-start(bf16[32,128,768]{2,1,0:T(8,128)(2,1)} %all-gather.5.cloned.1.call-done) | copy-start | bytes 18874372
  111.0 5.7 %copy-start.3 = (bf16[1,3072,256]{2,1,0:T(8,128)(2,1)S(1)}, bf16[1,3072,256]{2,1,0:T(8,128)(2,1)}, u32[]{:S(2)}) copy-start(bf16[1,3072,256]{2,1,0:T(8,128)(2,1)} %param.12) | copy-start | bytes 4718596
  204.1 1.9 copy-start.5
  204.1 1.9 copy-start.7
  204.1 1.9 copy-start.4
  220.9 8.8 %copy-start.8 = (bf16[8,128,256]{2,1,0:T(8,128)(2,1)S(1)}, bf16[8,128,256]{2,1,0:T(8,128)(2,1)}, u32[]{:S(2)}) copy-start(bf16[8,128,256]{2,1,0:T(8,128)(2,1)} %copy-done.7) | copy-start | bytes 1572868
  229.7 7.5 %copy-start.2 = (bf16[4,768,8,128]{3,1,0,2:T(8,128)(2,1)S(1)}, bf16[4,768,8,128]{3,1,0,2:T(8,128)(2,1)}, u32[]{:S(2)}) copy-start(bf16[4,768,8,128]{3,1,0,2:T(8,128)(2,1)} %copy.67) | copy-start | bytes 18874372
  229.7 7.5 %copy-start.9 = (f32[8,128,256]{2,1,0:T(8,128)S(1)}, f32[8,128,256]{2,1,0:T(8,128)}, u32[]{:S(2)}) copy-start(f32[8,128,256]{2,1,0:T(8,128)} %convolution_bitcast_fusion.3) | copy-start | bytes 3145732
  229.7 7.5 %copy-start.10 = (f32[8,128,256]{2,1,0:T(8,128)S(1)}, f32[8,128,256]{2,1,0:T(8,128)}, u32[]{:S(2)}) copy-start(f32[8,128,256]{2,1,0:T(8,128)} %convolution_bitcast_fusion.4) | copy-start | bytes 3145732
  237.2 220.1 %copy-start.6 = (bf16[8,128,256]{2,1,0:T(8,128)(2,1)S(1)}, bf16[8,128,256]{2,1,0:T(8,128)(2,1)}, u32[]{:S(2)}) copy-start(bf16[8,128,256]{2,1,0:T(8,128)(2,1)} %copy-done.5) | copy-start | bytes 1572868
  448.2 16.3 %all-to-all-start.2 = ((bf16[8,16,768]{2,1,0:T(8,128)(2,1)}), bf16[8,16,768]{2,1,0:T(8,128)(2,1)S(1)}, u32[]{:S(2)}, u32[]{:S(2)}) async-start(bf16[8,16,768]{2,1,0:T(8,128)(2,1)} %bitcast.24), calls=%async_computation.3 | async-start | bytes 393216 | tf_op jit(solution)/shard_map/all_to_all | solution.py:119
Sparse Core Ops, SparseCore 0:
  22.9 88.0 all-gather.4
  113.6 85.0 all-gather.2
  212.5 233.9 reduce-scatter.1
where the time goes:
time: 473 us; the launch traced here: 472 us
  waiting for transfers between devices  359 us (76%)
  matrix products  42.8 us (9%)
  blocking collectives  22 us (5%)
  local copies, waits for them, and re-layouts  21.8 us (5%)
  between operations  13.9 us (3%)
  starting transfers between devices  9.19 us (2%)
    reduce_scatter x1, waiting for transfers between devices, body(): lax.psum_scatter(input_terms.reshape(group_count * pipe_count, slot_total...  206 us
    all_gather x1, waiting for transfers between devices, body(): lax.all_gather(recv_grads.reshape(1, slot_total, feat_part), ('dp', 'pipe...  79.2 us
    all_gather x1, waiting for transfers between devices, body(): lax.all_gather(recv_rows.reshape(1, slot_total, feat_part), ('dp', 'pipe'...  73 us
    all_to_all x1, blocking collectives, body(): lax.all_to_all(sent_rows.reshape(expert_count, capacity, feat_part), 'exp...  12.1 us
    all_to_all x1, blocking collectives, body(): lax.all_to_all(sent_grads.reshape(expert_count, capacity, feat_part), 'ex...  9.87 us
  transfers between devices with their start and end apart: 4, of which 3 were waited for; matrix products, arithmetic and copies ran while one was open for 10% of the time, Pallas kernels for 0%

commit v1 on v0

--- a/solution.py
+++ b/solution.py
@@ -56,8 +56,16 @@
         ),
     )
     gathered_rows, gathered_gradients = (
-        lax.all_gather(
-            recv_rows.reshape(1, slot_total, feat_part), ("dp", "pipe"), axis=0, tiled=True
+        jnp.concatenate(
+            lax.all_to_all(
+                jnp.stack(
+                    [recv_rows.reshape(1, slot_total, feat_part)] * lax.axis_size(("dp", "pipe"))
+                ),
+                ("dp", "pipe"),
+                0,
+                0,
+            ),
+            axis=0,
         ),
         lax.all_gather(
             recv_grads.reshape(1, slot_total, feat_part), ("dp", "pipe"), axis=0, tiled=True

time: 473 us -> 508 us (1.074)
  waiting for transfers between devices: 359 us -> 384 us
  starting transfers between devices: 9.19 us -> 26.3 us
  blocking collectives: 22 us -> 9.19 us
    all_to_all x0 -> x2, waiting for transfers between devices: none -> 174 us  [the longest x1 170 us: body(): lax.all_to_all(jnp.stack([recv_rows.reshape(1, slot_total, feat_part)] *...]
    all_gather x1, waiting for transfers between devices: 79.2 us -> 0.01 us  [body(): lax.all_gather(recv_grads.reshape(1, slot_total, feat_part), ('dp', 'pipe...]
    all_gather x1 -> x0, waiting for transfers between devices: 73 us -> none  [body(): lax.all_gather(recv_rows.reshape(1, slot_total, feat_part), ('dp', 'pipe'...]
    all_to_all x0 -> x2, starting transfers between devices: none -> 17.2 us  [the longest x1 10.7 us: body(): lax.all_to_all(jnp.stack([recv_rows.reshape(1, slot_total, feat_part)] *...]
    all_to_all x1 -> x0, blocking collectives: 9.87 us -> none  [body(): lax.all_to_all(sent_grads.reshape(expert_count, capacity, feat_part), 'ex...]
  transfers between devices with their start and end apart: 4 -> 5, of which waited for: 3 -> 3; matrix products, arithmetic and copies ran while one was open for 10% -> 10% of each run, Pallas kernels for 0% -> 0%
where the time goes in v1:
time: 508 us; the launch traced here: 507 us
  waiting for transfers between devices  384 us (76%)
  matrix products  46.9 us (9%)
  starting transfers between devices  26.3 us (5%)
  local copies, waits for them, and re-layouts  23.7 us (5%)
  between operations  14.2 us (3%)
  blocking collectives  9.19 us (2%)
    reduce_scatter x1, waiting for transfers between devices, body(): lax.psum_scatter(input_terms.reshape(group_count * pipe_count, slot_total...  208 us
    all_to_all x1, waiting for transfers between devices, body(): lax.all_to_all(jnp.stack([recv_rows.reshape(1, slot_total, feat_part)] *...  170 us
    all_to_all x1, starting transfers between devices, body(): lax.all_to_all(jnp.stack([recv_rows.reshape(1, slot_total, feat_part)] *...  10.7 us
  transfers between devices with their start and end apart: 5, of which 3 were waited for; matrix products, arithmetic and copies ran while one was open for 10% of the time, Pallas kernels for 0%

profile of v1, /device:TPU:1, one launch (start us, length us, event | category | flops | bytes accessed | tf_op | source)
XLA Modules:
  0.0 507.4 jit_solution(504692900004145916)
XLA Ops:
  7.2 0.0 copy-start
  7.2 0.9 copy.50
  8.1 0.1 eq.30
  8.2 0.1 fusion.27
  8.2 0.1 reduce_window_sum.11
  8.3 0.2 select_reduce_fusion.1
  8.5 0.1 reduce_sum.21
  8.6 0.1 copy.51
  8.7 0.7 multiply_add_fusion
  9.4 0.8 select_reduce_fusion
  10.2 1.8 convolution_convert_fusion.1
  12.0 6.5 %all-to-all-start = ((bf16[8,16,768]{2,1,0:T(8,128)(2,1)}), bf16[8,16,768]{2,1,0:T(8,128)(2,1)S(1)}, u32[]{:S(2)}, u32[]{:S(2)}) async-start(bf16[8,16,768]{2,1,0:T(8,128)(2,1)} %bitcast), calls=%async_computation | async-start | bytes 393216 | tf_op jit(solution)/shard_map/all_to_all | solution.py:50
  18.5 0.1 fusion.28
  18.6 1.1 convolution_convert_fusion
  19.7 4.7 all-to-all-done
  24.4 9.2 %all_to_all.20 = bf16[8,16,768]{2,1,0:T(8,128)(2,1)S(1)} all-to-all(bf16[8,16,768]{2,1,0:T(8,128)(2,1)S(1)} %bitcast.117), channel_id=1, replica_groups=mesh['expert'=8,'dp'=8,'pipe'=4] {'expert'}, dimensions={0} | all-to-all | bytes 393216 | tf_op jit(solution)/shard_map/all_to_all | solution.py:43
  33.6 3.4 stack.3
  37.0 0.0 copy-done.8
  37.0 10.7 %all-to-all-start.2 = ((bf16[32,1,128,768]{3,2,1,0:T(8,128)(2,1)}), bf16[32,1,128,768]{3,2,1,0:T(8,128)(2,1)}, u32[]{:S(2)}, u32[]{:S(2)}) async-start(bf16[32,1,128,768]{3,2,1,0:T(8,128)(2,1)} %stack.3), calls=%async_computation.2 | async-start | bytes 12582912 | tf_op jit(solution)/shard_map/all_to_all | solution.py:60
  47.7 0.0 all-gather.2.cloned.1.call-start
  47.7 0.7 all-gather.2.cloned.1.call-update
  48.4 0.0 reduce-scatter.2.cloned.1.call-start
  48.5 0.0 copy-done.3
  48.5 2.1 reshape_squeeze.11
  50.6 169.6 %all-to-all-done.2 = bf16[32,1,128,768]{3,2,1,0:T(8,128)(2,1)} async-done(((bf16[32,1,128,768]{3,2,1,0:T(8,128)(2,1)}), bf16[32,1,128,768]{3,2,1,0:T(8,128)(2,1)}, u32[]{:S(2)}, u32[]{:S(2)}) %all-to-all-start.2) | async-done | bytes 6291488 | tf_op jit(solution)/shard_map/all_to_all | solution.py:60
  220.2 6.0 %fusion.16 = f32[8,128,256]{2,1,0:T(8,128)} fusion(bf16[4,768,256,1]{2,1,0,3:T(8,128)(2,1)} %bitcast.112, bf16[8,4,128,768]{3,2,1,0:T(8,128)(2,1)} %bitcast.101), kind=kOutput, calls=%fused_computation.18 | convolution fusion | flops 1610612736 | bytes 8912896 | tf_op jit(solution)/shard_map/lxvk,xkh->lvh/dot_general | solution.py:85
  226.2 0.0 copy-done
  226.2 5.7 %fusion.19 = f32[8,128,256]{2,1,0:T(8,128)} fusion(bf16[4,768,256,1]{2,1,0,3:T(8,128)(2,1)S(1)} %bitcast.104, bf16[8,4,128,768]{3,2,1,0:T(8,128)(2,1)} %bitcast.103), kind=kOutput, calls=%fused_computation.19 | convolution fusion | flops 1610612736 | bytes 8912896 | tf_op jit(solution)/shard_map/lxvk,xkh->lvh/dot_general | solution.py:82
  231.9 5.3 %multiply_convert_fusion.1 = (bf16[8,128,256]{2,1,0:T(8,128)(2,1)S(1)}, bf16[8,128,256]{2,1,0:T(8,128)(2,1)S(1)}) fusion(f32[8,128,256]{2,1,0:T(8,128)} %fusion.19, f32[8,128,256]{2,1,0:T(8,128)} %fusion.16, bf16[8,4,128,768]{3,2,1,0:T(8,128)(2,1)} %bitcast.107, bf16[256,4,768]{2,1,0:T(4,128)(2,1)S(1)} %copy-done.4), kind=kOutput, calls=%fused_computation.24 | convolution fusion | flops 1614020608 | bytes 11010048 | tf_op jit(solution)/shard_map/mzyj,uzj->myu/dot_general | solution.py:88
  237.2 0.0 copy-start.9
  237.2 0.0 copy-start.5
  237.3 1.8 fusion.24
  239.1 6.4 %convolution_add_fusion = f32[8,128,4,768]{3,1,2,0:T(8,128)} fusion(f32[8,128,4,768]{3,1,2,0:T(8,128)S(1)} %fusion.24, bf16[4,768,256,1]{2,1,0,3:T(8,128)(2,1)S(1)} %bitcast.113, bf16[8,128,256]{2,1,0:T(8,128)(2,1)S(1)} %get-tuple-element.4), kind=kOutput, calls=%fused_computation.4 | convolution fusion | flops 1613758464 | bytes 27262976 | tf_op jit(solution)/shard_map/mil,xkl->mxik/dot_general | solution.py:117
  245.5 0.0 reduce-scatter.2.cloned.1.call-update
  245.5 8.6 %copy.65 = bf16[4,768,8,128]{3,1,0,2:T(8,128)(2,1)} copy(bf16[4,768,8,128]{1,3,0,2:T(8,128)(2,1)} %bitcast.26) | data formatting | bytes 12582912 | tf_op jit(solution)/shard_map/kctx,ktn->cxn/dot_general | solution.py:97
  254.1 8.4 %copy.67 = bf16[4,768,8,128]{3,1,0,2:T(8,128)(2,1)} copy(bf16[4,768,8,128]{1,3,0,2:T(8,128)(2,1)} %bitcast.108) | data formatting | bytes 12582912 | tf_op jit(solution)/shard_map/cjb,cvji->bvi/dot_general | solution.py:109
  262.5 0.0 copy-start.12
  262.5 7.5 %fusion.8 = bf16[1,3072,256]{2,1,0:T(8,128)(2,1)} fusion(bf16[3072,8,128]{2,0,1:T(8,128)(2,1)} %bitcast.109, bf16[8,128,256]{2,1,0:T(8,128)(2,1)S(1)} %copy-done.10), kind=kOutput, calls=%fused_computation.12 | convolution fusion | flops 1611399168 | bytes 8388608 | tf_op jit(solution)/shard_map/kctx,ktn->cxn/dot_general | solution.py:103
  270.1 0.0 copy-done.2
  270.1 0.0 copy-done.12
  270.1 3.1 fusion.7
  273.2 208.4 %reduce-scatter.2.cloned.1.call-done = f32[1,128,768]{2,1,0:T(8,128)} async-done(((f32[32,128,768]{2,1,0:T(8,128)}), f32[1,128,768]{2,1,0:T(8,128)}) %reduce-scatter.2.cloned.1.call-update) | async-done | bytes 393232 | tf_op jit(solution)/shard_map/reduce_scatter | solution.py:120
  481.6 1.7 convert_element_type.40
  483.3 9.1 %all-to-all-start.3 = ((bf16[8,16,768]{2,1,0:T(8,128)(2,1)}), bf16[8,16,768]{2,1,0:T(8,128)(2,1)S(1)}, u32[]{:S(2)}, u32[]{:S(2)}) async-start(bf16[8,16,768]{2,1,0:T(8,128)(2,1)} %bitcast.24), calls=%async_computation.4 | async-start | bytes 393216 | tf_op jit(solution)/shard_map/all_to_all | solution.py:127
  492.4 0.0 copy-done.7
  492.4 7.4 %fusion.9 = bf16[1,3072,256]{2,1,0:T(8,128)(2,1)} fusion(bf16[3072,8,128]{2,0,1:T(8,128)(2,1)} %bitcast.110, bf16[8,128,256]{2,1,0:T(8,128)(2,1)S(1)} %copy-done.7), kind=kOutput, calls=%fused_computation.13 | convolution fusion | flops 1611399168 | bytes 8388608 | tf_op jit(solution)/shard_map/kctx,ktn->cxn/dot_general | solution.py:97
  499.8 0.0 all-to-all-done.3
  499.8 0.8 convolution_convert_fusion.2
  (17 shorter events, 0.0 us)
Async XLA Ops:
  7.2 219.1 %copy-start = (bf16[1,3072,256]{2,1,0:T(8,128)(2,1)S(1)}, bf16[1,3072,256]{2,1,0:T(8,128)(2,1)}, u32[]{:S(2)}) copy-start(bf16[1,3072,256]{2,1,0:T(8,128)(2,1)} %param.11) | copy-start | bytes 4718596
  12.0 12.4 %all-to-all-start = ((bf16[8,16,768]{2,1,0:T(8,128)(2,1)}), bf16[8,16,768]{2,1,0:T(8,128)(2,1)S(1)}, u32[]{:S(2)}, u32[]{:S(2)}) async-start(bf16[8,16,768]{2,1,0:T(8,128)(2,1)} %bitcast), calls=%async_computation | async-start | bytes 393216 | tf_op jit(solution)/shard_map/all_to_all | solution.py:50
  24.4 12.6 %copy-start.8 = (bf16[8,16,768]{2,1,0:T(8,128)(2,1)}, bf16[8,16,768]{2,1,0:T(8,128)(2,1)S(1)}, u32[]{:S(2)}) copy-start(bf16[8,16,768]{2,1,0:T(8,128)(2,1)S(1)} %all-to-all-done) | copy-start | bytes 589828
  37.0 11.5 %copy-start.3 = (bf16[1,256,3072]{2,1,0:T(8,128)(2,1)S(1)}, bf16[1,256,3072]{2,1,0:T(8,128)(2,1)}, u32[]{:S(2)}) copy-start(bf16[1,256,3072]{2,1,0:T(8,128)(2,1)} %param.13) | copy-start | bytes 4718596
  37.0 183.3 %all-to-all-start.2 = ((bf16[32,1,128,768]{3,2,1,0:T(8,128)(2,1)}), bf16[32,1,128,768]{3,2,1,0:T(8,128)(2,1)}, u32[]{:S(2)}, u32[]{:S(2)}) async-start(bf16[32,1,128,768]{3,2,1,0:T(8,128)(2,1)} %stack.3), calls=%async_computation.2 | async-start | bytes 12582912 | tf_op jit(solution)/shard_map/all_to_all | solution.py:60
  47.7 184.2 %all-gather.2.cloned.1.call-start = ((), (), s32[]{:S(2)}) async-start(), calls=%async_computation.5 | async-start | bytes 6488064 | tf_op jit(solution)/shard_map/all_gather | solution.py:70
  48.4 433.2 %reduce-scatter.2.cloned.1.call-start = ((), (), s32[]{:S(2)}) async-start(), calls=%async_computation.6 | async-start | bytes 12976128 | tf_op jit(solution)/shard_map/reduce_scatter | solution.py:120
  226.2 5.7 %copy-start.4 = (bf16[256,4,768]{2,1,0:T(4,128)(2,1)S(1)}, bf16[256,4,768]{2,1,0:T(4,128)(2,1)}, u32[]{:S(2)}) copy-start(bf16[256,4,768]{2,1,0:T(4,128)(2,1)} %reshape_squeeze.11) | copy-start | bytes 4718596
  237.2 1.9 copy-start.6
  237.2 1.9 copy-start.9
  237.2 1.9 copy-start.5
  254.1 8.4 %copy-start.10 = (bf16[8,128,256]{2,1,0:T(8,128)(2,1)S(1)}, bf16[8,128,256]{2,1,0:T(8,128)(2,1)}, u32[]{:S(2)}) copy-start(bf16[8,128,256]{2,1,0:T(8,128)(2,1)} %copy-done.9) | copy-start | bytes 1572868
  262.5 7.6 %copy-start.2 = (bf16[4,768,8,128]{3,1,0,2:T(8,128)(2,1)S(1)}, bf16[4,768,8,128]{3,1,0,2:T(8,128)(2,1)}, u32[]{:S(2)}) copy-start(bf16[4,768,8,128]{3,1,0,2:T(8,128)(2,1)} %copy.67) | copy-start | bytes 18874372
  262.5 7.6 %copy-start.11 = (f32[8,128,256]{2,1,0:T(8,128)S(1)}, f32[8,128,256]{2,1,0:T(8,128)}, u32[]{:S(2)}) copy-start(f32[8,128,256]{2,1,0:T(8,128)} %fusion.16) | copy-start | bytes 3145732
  262.5 7.6 %copy-start.12 = (f32[8,128,256]{2,1,0:T(8,128)S(1)}, f32[8,128,256]{2,1,0:T(8,128)}, u32[]{:S(2)}) copy-start(f32[8,128,256]{2,1,0:T(8,128)} %fusion.19) | copy-start | bytes 3145732
  270.1 222.3 %copy-start.7 = (bf16[8,128,256]{2,1,0:T(8,128)(2,1)S(1)}, bf16[8,128,256]{2,1,0:T(8,128)(2,1)}, u32[]{:S(2)}) copy-start(bf16[8,128,256]{2,1,0:T(8,128)(2,1)} %copy-done.6) | copy-start | bytes 1572868
  483.3 16.5 %all-to-all-start.3 = ((bf16[8,16,768]{2,1,0:T(8,128)(2,1)}), bf16[8,16,768]{2,1,0:T(8,128)(2,1)S(1)}, u32[]{:S(2)}, u32[]{:S(2)}) async-start(bf16[8,16,768]{2,1,0:T(8,128)(2,1)} %bitcast.24), calls=%async_computation.4 | async-start | bytes 393216 | tf_op jit(solution)/shard_map/all_to_all | solution.py:127
  492.4 8.2 %copy-start.1 = (bf16[1,3072,256]{2,1,0:T(8,128)(2,1)S(1)}, bf16[1,3072,256]{2,1,0:T(8,128)(2,1)}, u32[]{:S(2)}) copy-start(bf16[1,3072,256]{2,1,0:T(8,128)(2,1)} %param.11) | copy-start | bytes 4718596
Sparse Core Ops, SparseCore 0:
  51.7 169.8 all-gather.1
  245.6 235.9 reduce-scatter.1
